TPU v7x, 32 devices: a whole 2x2x4 slice. The times are simulated.
32 devices in a mesh: sect: 2 (over y), op: 16 (over z, x, core).
Axes of the slice: x: 2, y: 2, z: 4, core: 2. Of those that a mesh axis runs over, the one named last changes fastest.
Arguments:
- wave: bfloat16 [2, 8192, 256], P('sect', 'op'), may hold values from -6 to 6
- left_ops: bfloat16 [2, 48, 8, 256, 256], P('sect', 'op'), may hold values from -0.5 to 0.5
- right_ops: bfloat16 [2, 48, 8, 256, 256], P('sect', 'op'), may hold values from -0.375 to 0.375
- site_ops: float32 [2, 48, 4, 4], P('sect', 'op'), may hold values from -0.4375 to 0.4375
- reach: int32 [2, 48], P('sect', 'op'), may hold values from 1 to 8
- pairing: int32 [2, 8], P('sect'), may hold values from 0 to 7, each once within a row
- site_tensor: bfloat16 [2, 8, 4, 256, 256], P('sect'), may hold values from -0.25 to 0.25
Outputs:
- first_image: bfloat16 [2, 8192, 256], P('sect', 'op')
- second_image: bfloat16 [2, 8192, 256], P('sect', 'op')
- moved_image: bfloat16 [2, 8192, 256], P('sect', 'op')
Inputs may be any that keep to these rules, and one draw needn't show every extreme that they name: Each term couples the sectors 0 to reach - 1. `pairing`: each row is a permutation of the 8 sectors.
All inputs are finite; a program needn't handle non-finite values.
Results may differ from a plain program's by a relative error of at most 0.008.
Values may be sent and summed in bfloat16 or wider, within the bound.
A program may use at most 128 MiB of HBM per device.

v0:
```python
import jax
import jax.numpy as jnp
from jax import lax
from jax.sharding import PartitionSpec as P


def from_behind(value, axis, steps):
    count = lax.axis_size(axis)
    pairs = [(source, (source + steps) % count) for source in range(count)]
    return lax.ppermute(value, axis, pairs)


def apply_local(rows, lefts, rights, mixers, limits, pair):
    sectors = lefts.shape[1]
    block = lefts.shape[2]
    local = mixers.shape[1]
    blocks = rows.reshape(sectors, local, block, block)
    sector_ids = jnp.arange(sectors, dtype=jnp.int32)
    total = jnp.zeros(blocks.shape, jnp.float32)
    for term in range(lefts.shape[0]):
        lifted = jnp.einsum(
            "qab,qsbc->qsac", lefts[term], blocks, preferred_element_type=jnp.float32
        ).astype(jnp.bfloat16)
        mask = (sector_ids < limits[term]).astype(jnp.float32)
        mixed = jnp.einsum(
            "xy,qyac->qxac",
            mixers[term],
            lifted.astype(jnp.float32),
            precision=lax.Precision.HIGHEST,
        )
        mixed = (mixed * mask[:, None, None, None]).astype(jnp.bfloat16)
        paired = jnp.take(rights[term], pair, axis=0)
        total = total + jnp.einsum(
            "qsac,qdc->qsad", mixed, paired, preferred_element_type=jnp.float32
        )
    return total.reshape(rows.shape)


def renew_boundary(lefts, tensor, pair):
    sectors = lefts.shape[1]
    onehot = (pair[:, None] == jnp.arange(sectors, dtype=jnp.int32)[None, :]).astype(jnp.bfloat16)
    placed_all = []
    for term in range(lefts.shape[0]):
        lifted = jnp.einsum(
            "qab,qsbc->qsac", lefts[term], tensor, preferred_element_type=jnp.float32
        ).astype(jnp.bfloat16)
        reduced = jnp.einsum(
            "qsad,qsac->qdc", tensor, lifted, preferred_element_type=jnp.float32
        ).astype(jnp.bfloat16)
        placed = jnp.einsum("qj,qdc->jdc", onehot, reduced, preferred_element_type=jnp.float32)
        placed_all.append(placed.astype(jnp.bfloat16))
    renewed = jnp.stack(placed_all)
    return from_behind(renewed, "sect", 1)


def shards(wave, left_ops, right_ops, site_ops, reach, pairing, site_tensor):
    lefts = left_ops[0]
    rights = right_ops[0]
    mixers = site_ops[0]
    limits = reach[0]
    pair = pairing[0]
    whole = lax.all_gather(wave[0], "op", axis=0, tiled=True)
    first_part = apply_local(whole, lefts, rights, mixers, limits, pair)
    first_own = lax.psum_scatter(first_part, "op", scatter_dimension=0, tiled=True).astype(
        jnp.bfloat16
    )
    first_full = lax.all_gather(first_own, "op", axis=0, tiled=True)
    moved_lefts = renew_boundary(lefts, site_tensor[0], pair)
    second_part = apply_local(first_full, lefts, rights, mixers, limits, pair)
    second_own = lax.psum_scatter(second_part, "op", scatter_dimension=0, tiled=True).astype(
        jnp.bfloat16
    )
    moved_part = apply_local(whole, moved_lefts, rights, mixers, limits, pair)
    moved_own = lax.psum_scatter(moved_part, "op", scatter_dimension=0, tiled=True).astype(
        jnp.bfloat16
    )
    return (first_own[None], second_own[None], moved_own[None])


def solution(mesh):
    placed = (
        P("sect", "op", None),
        P("sect", "op", None, None, None),
        P("sect", "op", None, None, None),
        P("sect", "op", None, None),
        P("sect", "op"),
        P("sect", None),
        P("sect", None, None, None, None),
    )
    return jax.shard_map(
        shards,
        mesh=mesh,
        in_specs=placed,
        out_specs=(P("sect", "op", None), P("sect", "op", None), P("sect", "op", None)),
        check_vma=False,
    )
```

profile of v0, /device:TPU:0, one launch (start us, length us, event | category | flops | bytes accessed | tf_op | source)
XLA Modules:
  0.0 556.7 jit_solution(10205782150317037963)
XLA Ops:
  17.4 45.9 %all-gather.6.cloned.1.call-done = bf16[1,8192,256]{2,1,0:T(8,128)(2,1)} async-done(((bf16[1,512,256]{2,1,0:T(8,128)(2,1)}), bf16[1,8192,256]{2,1,0:T(8,128)(2,1)}) %all-gather.6.cloned.1.call-update) | async-done | bytes 4194320 | tf_op jit(solution)/shard_map/all_gather | solution.py:62
  76.4 7.6 %copy.11 = bf16[8,4,256,256]{3,1,2,0:T(4,128)(2,1)} copy(bf16[8,4,256,256]{2,3,1,0:T(8,128)(2,1)} %convert_bitcast_fusion.5) | data formatting | bytes 8388608 | tf_op jit(solution)/shard_map/convert_element_type | solution.py:23
  83.9 7.4 %copy.16 = bf16[8,4,256,256]{3,1,2,0:T(4,128)(2,1)} copy(bf16[8,4,256,256]{2,3,1,0:T(8,128)(2,1)} %convert_bitcast_fusion.4) | data formatting | bytes 8388608 | tf_op jit(solution)/shard_map/convert_element_type | solution.py:23
  91.4 10.7 %fusion.146 = f32[8,256,256,4]{2,3,1,0:T(4,128)} fusion(bf16[8,4,256,256]{3,1,2,0:T(4,128)(2,1)} %copy.11, f32[1,3,4,4]{3,2,1,0:T(4,128)S(1)} %copy-done.7), kind=kOutput, calls=%fused_computation.155 | convolution fusion | flops 100663296 | bytes 12584960 | tf_op jit(solution)/shard_map/xy,qyac->qxac/dot_general | solution.py:25
  102.1 8.9 %fusion.141 = f32[8,256,256,4]{2,3,1,0:T(4,128)} fusion(bf16[8,4,256,256]{3,1,2,0:T(4,128)(2,1)S(1)} %copy-done.3, f32[1,3,4,4]{3,2,1,0:T(4,128)S(1)} %copy-done.7), kind=kOutput, calls=%fused_computation.150 | convolution fusion | flops 100663296 | bytes 12584960 | tf_op jit(solution)/shard_map/xy,qyac->qxac/dot_general | solution.py:25
  111.0 7.4 %copy.21 = bf16[8,4,256,256]{3,1,2,0:T(4,128)(2,1)} copy(bf16[8,4,256,256]{2,3,1,0:T(8,128)(2,1)} %convert_bitcast_fusion.3) | data formatting | bytes 8388608 | tf_op jit(solution)/shard_map/convert_element_type | solution.py:23
  118.4 10.8 %fusion.136 = f32[8,256,256,4]{2,3,1,0:T(4,128)} fusion(bf16[8,4,256,256]{3,1,2,0:T(4,128)(2,1)} %copy.21, f32[1,3,4,4]{3,2,1,0:T(4,128)S(1)} %copy-done.7), kind=kOutput, calls=%fused_computation.145 | convolution fusion | flops 100663296 | bytes 12584960 | tf_op jit(solution)/shard_map/xy,qyac->qxac/dot_general | solution.py:25
  129.2 8.4 %fusion.10 = f32[8,4,256,256]{3,2,1,0:T(8,128)} fusion(f32[8,256,256,4]{2,3,1,0:T(4,128)} %fusion.146, f32[8]{0:T(128)S(1)} %compare_convert_fusion.2, bf16[8,256,256]{2,1,0:T(8,128)(2,1)S(1)} %gather_fusion, pred[8]{0:T(512)(128)(4,1)S(1)} %compare_and_fusion), kind=kOutput, calls=%fused_computation.25 | convolution fusion | flops 1078460416 | bytes 17825832 | tf_op jit(solution)/shard_map/qsac,qdc->qsad/dot_general | solution.py:33
  142.6 14.0 %add_add_fusion.2 = f32[8,4,256,256]{3,2,1,0:T(8,128)} fusion(f32[8,4,256,256]{3,2,1,0:T(8,128)} %fusion.10, f32[8,4,256,256]{3,2,1,0:T(8,128)} %fusion.13, f32[8,256,256,4]{2,3,1,0:T(4,128)} %fusion.136, f32[8]{0:T(128)S(1)} %compare_convert_fusion, bf16[8,256,256]{2,1,0:T(8,128)(2,1)S(1)} %gather_fusion.2, pred[8]{0:T(512)(128)(4,1)S(1)} %compare_and_fusion), kind=kOutput, calls=%fused_computation.23 | convolution fusion | flops 1082654720 | bytes 34603048 | tf_op jit(solution)/shard_map/qsac,qdc->qsad/dot_general | solution.py:33
  166.9 8.0 %fusion.41 = bf16[8,256,256,1]{2,1,3,0:T(8,128)(2,1)} fusion(bf16[1,8,4,256,256]{4,3,2,1,0:T(8,128)(2,1)} %param.15, bf16[1,3,8,256,256]{4,3,2,1,0:T(8,128)(2,1)} %param.10), kind=kOutput, calls=%fused_computation.50 | convolution fusion | flops 2149580800 | bytes 10485760 | tf_op jit(solution)/shard_map/qsad,qsac->qdc/dot_general | solution.py:47
  177.6 7.2 %fusion.43 = bf16[8,256,256,1]{2,1,3,0:T(8,128)(2,1)} fusion(bf16[1,8,4,256,256]{4,3,2,1,0:T(8,128)(2,1)} %param.15, bf16[1,3,8,256,256]{4,3,2,1,0:T(8,128)(2,1)} %param.10), kind=kOutput, calls=%fused_computation.52 | convolution fusion | flops 2149580800 | bytes 10485760 | tf_op jit(solution)/shard_map/qsad,qsac->qdc/dot_general | solution.py:47
  194.8 63.9 %reduce-scatter.4.cloned.1.call-done = f32[512,256]{1,0:T(8,128)} async-done(((f32[8192,256]{1,0:T(8,128)}), f32[512,256]{1,0:T(8,128)}) %reduce-scatter.4.cloned.1.call-update) | async-done | bytes 524304 | tf_op jit(solution)/shard_map/reduce_scatter | solution.py:64
  271.7 14.8 %fusion.38 = f32[8,256,256,4]{2,3,1,0:T(4,128)S(1)} fusion(bf16[8,256,4,256]{3,1,2,0:T(8,128)(2,1)S(1)} %convolution_convert_fusion.2, f32[1,3,4,4]{3,2,1,0:T(4,128)S(1)} %copy-done.7), kind=kOutput, calls=%fused_computation.47 | convolution fusion | flops 100663296 | bytes 12584960 | tf_op jit(solution)/shard_map/xy,qyac->qxac/dot_general | solution.py:25
  286.5 14.6 %fusion.37 = f32[8,256,256,4]{2,3,1,0:T(4,128)S(1)} fusion(bf16[8,256,4,256]{3,1,2,0:T(8,128)(2,1)S(1)} %convolution_convert_fusion.1, f32[1,3,4,4]{3,2,1,0:T(4,128)S(1)} %copy-done.7), kind=kOutput, calls=%fused_computation.45 | convolution fusion | flops 100663296 | bytes 12584960 | tf_op jit(solution)/shard_map/xy,qyac->qxac/dot_general | solution.py:25
  301.2 13.5 %fusion.36 = f32[8,256,256,4]{2,3,1,0:T(4,128)} fusion(bf16[8,256,4,256]{3,1,2,0:T(8,128)(2,1)} %convolution_convert_fusion, f32[1,3,4,4]{3,2,1,0:T(4,128)S(1)} %copy-done.7), kind=kOutput, calls=%fused_computation.43 | convolution fusion | flops 100663296 | bytes 12584960 | tf_op jit(solution)/shard_map/xy,qyac->qxac/dot_general | solution.py:25
  324.4 14.0 %add_add_fusion = f32[8,4,256,256]{3,2,1,0:T(8,128)} fusion(f32[8,4,256,256]{3,2,1,0:T(8,128)} %fusion.28, f32[8,4,256,256]{3,2,1,0:T(8,128)} %fusion.31, f32[8,256,256,4]{2,3,1,0:T(4,128)} %fusion.36, f32[8]{0:T(128)S(1)} %compare_convert_fusion, bf16[8,256,256]{2,1,0:T(8,128)(2,1)S(1)} %gather_fusion.2, pred[8]{0:T(512)(128)(4,1)S(1)} %compare_and_fusion), kind=kOutput, calls=%fused_computation.21 | convolution fusion | flops 1082654720 | bytes 34603048 | tf_op jit(solution)/shard_map/qsac,qdc->qsad/dot_general | solution.py:33
  344.8 7.8 %copy.25 = bf16[8,4,256,256]{3,1,2,0:T(4,128)(2,1)} copy(bf16[8,4,256,256]{2,3,1,0:T(8,128)(2,1)} %convert_bitcast_fusion.2) | data formatting | bytes 8388608 | tf_op jit(solution)/shard_map/convert_element_type | solution.py:23
  359.1 7.5 %copy.27 = bf16[8,4,256,256]{3,1,2,0:T(4,128)(2,1)} copy(bf16[8,4,256,256]{2,3,1,0:T(8,128)(2,1)} %convert_bitcast_fusion.1) | data formatting | bytes 8388608 | tf_op jit(solution)/shard_map/convert_element_type | solution.py:23
  372.6 7.4 %copy.29 = bf16[8,4,256,256]{3,1,2,0:T(4,128)(2,1)} copy(bf16[8,4,256,256]{2,3,1,0:T(8,128)(2,1)} %convert_bitcast_fusion) | data formatting | bytes 8388608 | tf_op jit(solution)/shard_map/convert_element_type | solution.py:23
  380.0 8.6 %fusion.144 = f32[8,256,256,4]{2,3,1,0:T(4,128)S(1)} fusion(bf16[8,4,256,256]{3,1,2,0:T(4,128)(2,1)} %copy.25, f32[1,3,4,4]{3,2,1,0:T(4,128)S(1)} %copy-done.7), kind=kOutput, calls=%fused_computation.153 | convolution fusion | flops 100663296 | bytes 12584960 | tf_op jit(solution)/shard_map/xy,qyac->qxac/dot_general | solution.py:25
  395.7 10.7 %fusion.134 = f32[8,256,256,4]{2,3,1,0:T(4,128)} fusion(bf16[8,4,256,256]{3,1,2,0:T(4,128)(2,1)} %copy.29, f32[1,3,4,4]{3,2,1,0:T(4,128)S(1)} %copy-done.7), kind=kOutput, calls=%fused_computation.143 | convolution fusion | flops 100663296 | bytes 12584960 | tf_op jit(solution)/shard_map/xy,qyac->qxac/dot_general | solution.py:25
  416.2 14.4 %add_add_fusion.1 = f32[8,4,256,256]{3,2,1,0:T(8,128)} fusion(f32[8,4,256,256]{3,2,1,0:T(8,128)} %fusion.19, f32[8,4,256,256]{3,2,1,0:T(8,128)} %fusion.22, f32[8,256,256,4]{2,3,1,0:T(4,128)} %fusion.134, f32[8]{0:T(128)S(1)} %compare_convert_fusion, bf16[8,256,256]{2,1,0:T(8,128)(2,1)S(1)} %gather_fusion.2, pred[8]{0:T(512)(128)(4,1)S(1)} %compare_and_fusion), kind=kOutput, calls=%fused_computation.22 | convolution fusion | flops 1082654720 | bytes 34603048 | tf_op jit(solution)/shard_map/qsac,qdc->qsad/dot_general | solution.py:33
  432.3 8.8 %reduce-scatter.8.cloned.1.call-done = f32[512,256]{1,0:T(8,128)} async-done(((f32[8192,256]{1,0:T(8,128)}), f32[512,256]{1,0:T(8,128)}) %reduce-scatter.8.cloned.1.call-update) | async-done | bytes 524304 | tf_op jit(solution)/shard_map/reduce_scatter | solution.py:74
  442.9 105.2 %reduce-scatter.6.cloned.1.call-done = f32[512,256]{1,0:T(8,128)} async-done(((f32[8192,256]{1,0:T(8,128)}), f32[512,256]{1,0:T(8,128)}) %reduce-scatter.6.cloned.1.call-update) | async-done | bytes 524304 | tf_op jit(solution)/shard_map/reduce_scatter | solution.py:70
  (77 shorter events, 114.9 us)
Async XLA Ops:
  7.2 56.1 %all-gather.6.cloned.1.call-start = ((), (), s32[]{:S(2)}) async-start(), calls=%async_computation.7 | async-start | bytes 4456448 | tf_op jit(solution)/shard_map/all_gather | solution.py:62
  7.9 250.8 %reduce-scatter.4.cloned.1.call-start = ((), (), s32[]{:S(2)}) async-start(), calls=%async_computation.3 | async-start | bytes 8912896 | tf_op jit(solution)/shard_map/reduce_scatter | solution.py:64
  11.7 3.1 copy-start.9
  11.7 5.7 %copy-start.8 = (s32[1,8]{1,0:T(1,128)S(1)}, s32[1,8]{1,0:T(1,128)}, u32[]{:S(2)}) copy-start(s32[1,8]{1,0:T(1,128)} %param.14) | copy-start | bytes 100
  63.3 6.1 %copy-start = (bf16[1,8192,256]{2,1,0:T(8,128)(2,1)S(1)}, bf16[1,8192,256]{2,1,0:T(8,128)(2,1)}, u32[]{:S(2)}) copy-start(bf16[1,8192,256]{2,1,0:T(8,128)(2,1)} %all-gather.6.cloned.1.call-done) | copy-start | bytes 12582916
  63.3 6.1 %copy-start.4 = (bf16[1,3,8,256,256]{4,3,2,1,0:T(8,128)(2,1)S(1)}, bf16[1,3,8,256,256]{4,3,2,1,0:T(8,128)(2,1)}, u32[]{:S(2)}) copy-start(bf16[1,3,8,256,256]{4,3,2,1,0:T(8,128)(2,1)} %param.10) | copy-start | bytes 9437188
  83.9 7.4 %copy-start.7 = (f32[1,3,4,4]{3,2,1,0:T(4,128)S(1)}, f32[1,3,4,4]{3,2,1,0:T(4,128)}, u32[]{:S(2)}) copy-start(f32[1,3,4,4]{3,2,1,0:T(4,128)} %param.12) | copy-start | bytes 580
  91.4 10.7 %copy-start.3 = (bf16[8,4,256,256]{3,1,2,0:T(4,128)(2,1)S(1)}, bf16[8,4,256,256]{3,1,2,0:T(4,128)(2,1)}, u32[]{:S(2)}) copy-start(bf16[8,4,256,256]{3,1,2,0:T(4,128)(2,1)} %copy.16) | copy-start | bytes 12582916
  118.4 19.3 %slice-start = ((s8[8388608]{0:T(1024)(128)(4,1)}), s8[4194304]{0:T(1024)(128)(4,1)S(1)}, s32[]{:S(2)}) async-start(s8[8388608]{0:T(1024)(128)(4,1)} %bitcast.279), calls=%async_computation.8 | async-start | bytes 8388608
  129.2 8.4 %slice-start.1 = ((s8[8388608]{0:T(1024)(128)(4,1)}), s8[4194304]{0:T(1024)(128)(4,1)S(1)}, s32[]{:S(2)}) async-start(s8[8388608]{0:T(1024)(128)(4,1)} %bitcast.279), calls=%async_computation.9 | async-start | bytes 8388608
  156.6 182.3 %all-gather.4.cloned.1.call-start = ((), (), s32[]{:S(2)}) async-start(), calls=%async_computation.4 | async-start | bytes 4456448 | tf_op jit(solution)/shard_map/all_gather | solution.py:67
  187.4 3.4 copy-start.5
  193.3 70.6 %collective-permute-start = (bf16[3,8,256,256]{3,1,2,0:T(8,128)(2,1)}, bf16[3,8,256,256]{3,1,2,0:T(8,128)(2,1)}, u32[]{:S(2)}, u32[]{:S(2)}) collective-permute-start(bf16[3,8,256,256]{3,1,2,0:T(8,128)(2,1)} %pad_maximum_fusion), channel_id=1, source_target_pairs={{0,16},{16,0},{1,17},{17,1},{2,18},{18,2},{3,19},{19,3},{4,20},{20... | collective-permute-start | bytes 9437192 | tf_op jit(solution)/shard_map/ppermute | solution.py:10
  260.5 180.7 %reduce-scatter.8.cloned.1.call-start = ((), (), s32[]{:S(2)}) async-start(), calls=%async_computation.6 | async-start | bytes 8912896 | tf_op jit(solution)/shard_map/reduce_scatter | solution.py:74
  260.6 5.4 copy-start.1
  338.4 209.7 %reduce-scatter.6.cloned.1.call-start = ((), (), s32[]{:S(2)}) async-start(), calls=%async_computation.5 | async-start | bytes 8912896 | tf_op jit(solution)/shard_map/reduce_scatter | solution.py:70
  380.0 8.6 %copy-start.2 = (bf16[8,4,256,256]{3,1,2,0:T(4,128)(2,1)S(1)}, bf16[8,4,256,256]{3,1,2,0:T(4,128)(2,1)}, u32[]{:S(2)}) copy-start(bf16[8,4,256,256]{3,1,2,0:T(4,128)(2,1)} %copy.27) | copy-start | bytes 12582916
  430.6 1.0 copy-start.6
Sparse Core Ops, SparseCore 0:
  10.1 53.0 all-gather.5
  156.7 101.9 reduce-scatter.3
  261.5 50.0 all-gather.3
  338.6 102.5 reduce-scatter.7
  445.1 103.0 reduce-scatter.5
where the time goes:
time: 562 us; the launch traced here: 557 us
  matrix products  238 us (42%)
  waiting for transfers between devices  228 us (41%)
  local copies, waits for them, and re-layouts  63.4 us (11%)
  between operations  14.2 us (3%)
  other arithmetic  10.7 us (2%)
    reduce_scatter x1, waiting for transfers between devices, shards(): lax.psum_scatter(second_part, 'op', scatter_dimension=0, tiled=True)  105 us
    dot_general x9, matrix products, apply_local(): jnp.einsum('xy,qyac->qxac', mixers[term], lifted.astype(jnp.float32), pre...  99.7 us
    dot_general x9, matrix products, apply_local(): jnp.einsum('qsac,qdc->qsad', mixed, paired, preferred_element_type=jnp.fl...  75.2 us
    reduce_scatter x1, waiting for transfers between devices, shards(): lax.psum_scatter(first_part, 'op', scatter_dimension=0, tiled=True)  63.9 us
    all_gather x1, waiting for transfers between devices, shards(): whole = lax.all_gather(wave[0], 'op', axis=0, tiled=True)  45.9 us
    convert_element_type x6, local copies, waits for them, and re-layouts, apply_local(): lifted = jnp.einsum('qab,qsbc->qsac', lefts[term], blocks, preferred_elem...  45.1 us
    dot_general x9, matrix products, apply_local(): jnp.einsum('qab,qsbc->qsac', lefts[term], blocks, preferred_element_type=...  37.3 us
    dot_general x3, matrix products, renew_boundary(): jnp.einsum('qsad,qsac->qdc', tensor, lifted, preferred_element_type=jnp.f...  22.4 us
  transfers between devices with their start and end apart: 6, of which 5 were waited for; matrix products, arithmetic and copies ran while one was open for 39% of the time, Pallas kernels for 0%

commit v1 on v0

v1 whole, which is shorter than its diff:
```python
import functools

import jax
import jax.numpy as jnp
from jax import lax
from jax.experimental import pallas as pl
from jax.experimental.pallas import tpu as pltpu
from jax.sharding import PartitionSpec as P

VM = pl.BlockSpec(memory_space=pltpu.VMEM)
SUBS = 2
BIG = 64000 * 1024


class Ring:
    def __init__(self, count):
        me = lax.axis_index("op")
        self.m = count // 2
        self.half = self.m // 2
        self.core = lax.rem(me, 2)
        self.chip = lax.div(me, 2)
        odd = lax.rem(self.chip, 2)
        low = lax.div(self.chip, 2)
        self.pos = (1 - odd) * low + odd * (self.m - 1 - low)
        self.sibling = {"op": self.chip * 2 + 1 - self.core}
        self.next = [
            {"op": self.chip_at(1) * 2 + self.core},
            {"op": self.chip_at(-1) * 2 + self.core},
        ]

    def chip_at(self, offset):
        pos = lax.rem(self.pos + offset + self.m, self.m)
        upper = lax.div(pos, self.half)
        return (1 - upper) * (2 * pos) + upper * (2 * (self.m - 1 - pos) + 1)

    def barrier(self):
        sem = pltpu.get_barrier_semaphore()
        for who in (self.next[0], self.next[1], self.sibling):
            pl.semaphore_signal(sem, inc=1, device_id=who, device_id_type=pl.DeviceIdType.MESH)
        pl.semaphore_wait(sem, 3)


def push(src, dst, send, recv, who):
    copy = pltpu.make_async_remote_copy(
        src_ref=src, dst_ref=dst, send_sem=send, recv_sem=recv, device_id=who,
        device_id_type=pl.DeviceIdType.MESH,
    )
    copy.start()
    return copy


def scatter_sum(ring, streams):
    m, half = ring.m, ring.half
    order = [half]
    for dist in range(half - 1, 0, -1):
        order += [dist, -dist]
    order.append(0)
    sent = []
    sib = {}
    for slot, offset in enumerate(order):
        chunk = ring.chip_at(offset)
        for n, st in enumerate(streams):
            sib[n, offset] = push(
                st["give"].at[chunk], st["land"].at[chunk], st["sib_send"].at[slot],
                st["sib_recv"].at[slot], ring.sibling,
            )
    arrived = set()
    hops = {}

    def local(n, offset, u):
        st = streams[n]
        if (n, offset) not in arrived:
            arrived.add((n, offset))
            sib[n, offset].wait_recv()
        chunk = ring.chip_at(offset)
        rows = st["own"].shape[1] // SUBS
        cut = pl.ds(u * rows, rows)
        return st["own"][chunk, cut, :] + st["land"][chunk, cut, :].astype(jnp.float32)

    def incoming(n, d, j, u):
        hops[n, d, j, u].wait_recv()
        return streams[n]["rbuf"][d, j, u].astype(jnp.float32)

    for j in range(half):
        dist = half - j
        for n, st in enumerate(streams):
            for u in range(SUBS):
                for d in range(2):
                    if dist == half and u != d:
                        continue
                    offset = dist if (d == 0 or dist == half) else -dist
                    value = local(n, offset, u)
                    if (n, d, j - 1, u) in hops:
                        value = value + incoming(n, d, j - 1, u)
                    st["sbuf"][d, j, u] = value.astype(jnp.bfloat16)
                    hops[n, d, j, u] = push(
                        st["sbuf"].at[d, j, u], st["rbuf"].at[d, j, u],
                        st["send"].at[d, j, u], st["recv"].at[d, j, u], ring.next[d],
                    )
    for n, st in enumerate(streams):
        for u in range(SUBS):
            value = local(n, 0, u)
            for d in range(2):
                if (n, d, half - 1, u) in hops:
                    value = value + incoming(n, d, half - 1, u)
            rows = value.shape[0]
            st["out"][pl.ds(u * rows, rows), :] = value.astype(jnp.bfloat16)
    sent += list(sib.values()) + list(hops.values())
    return sent


def gather(ring, own, whole, send, recv, sib_send, sib_recv):
    half = ring.half
    rows = own.shape[0] // SUBS
    sent, sib, hops = [], [], {}

    def part(chunk, u):
        return whole.at[chunk, ring.core, pl.ds(u * rows, rows)]

    def to_sibling(src, chunk, u):
        slot = len(sib)
        sib.append(push(src, part(chunk, u), sib_send.at[slot], sib_recv.at[slot], ring.sibling))

    for s in range(half + 1):
        for u in range(SUBS):
            for d in range(2):
                chunk = ring.chip_at(-s if d == 0 else s)
                if s == 0:
                    src = own.at[pl.ds(u * rows, rows)]
                else:
                    if (d, s - 1, u) not in hops:
                        continue
                    hops[d, s - 1, u].wait_recv()
                    src = part(chunk, u)
                if s < half and (s < half - 1 or u == d):
                    hops[d, s, u] = push(
                        src, part(chunk, u), send.at[d, s, u], recv.at[d, s, u], ring.next[d]
                    )
                if s > 0 or d == 0:
                    to_sibling(src, chunk, u)
    for copy in sib:
        copy.wait_recv()
    return sib + list(hops.values())


def gather_kernel(count, own, whole, send, recv, sib_send, sib_recv, local_sem):
    ring = Ring(count)
    ring.barrier()
    keep = pltpu.make_async_copy(own, whole.at[ring.chip, ring.core], local_sem)
    keep.start()
    sent = gather(ring, own, whole, send, recv, sib_send, sib_recv)
    for copy in sent:
        copy.wait_send()
    keep.wait()


def reduce_kernel(count, streams, regather, *refs):
    refs = list(refs)
    take = lambda n: [refs.pop(0) for _ in range(n)]
    ins = take(2 * streams)
    outs = take(streams)
    whole = take(1)[0] if regather else None
    made = []
    for n in range(streams):
        land, sbuf, rbuf, send, recv, sib_send, sib_recv = take(7)
        made.append(dict(
            own=ins[2 * n], give=ins[2 * n + 1], out=outs[n], land=land, sbuf=sbuf, rbuf=rbuf,
            send=send, recv=recv, sib_send=sib_send, sib_recv=sib_recv,
        ))
    ring = Ring(count)
    ring.barrier()
    sent = scatter_sum(ring, made)
    if regather:
        send, recv, sib_send, sib_recv, local_sem = take(5)
        keep = pltpu.make_async_copy(outs[0], whole.at[ring.chip, ring.core], local_sem)
        keep.start()
        sent += gather(ring, outs[0], whole, send, recv, sib_send, sib_recv)
        keep.wait()
    for copy in sent:
        copy.wait_send()


def gather_scratch(count):
    half = count // 4
    dma = pltpu.SemaphoreType.DMA
    slots = SUBS * (2 * half)
    return [dma((2, half, SUBS)), dma((2, half, SUBS)), dma((slots,)), dma((slots,)), dma]


def all_gather(own, count, ident):
    rows, width = own.shape
    whole = pl.pallas_call(
        functools.partial(gather_kernel, count),
        out_shape=jax.ShapeDtypeStruct((count // 2, 2, rows, width), own.dtype),
        in_specs=[VM],
        out_specs=VM,
        scratch_shapes=gather_scratch(count),
        compiler_params=pltpu.CompilerParams(
            collective_id=ident, has_side_effects=True, vmem_limit_bytes=BIG
        ),
        name="gather_rows",
    )(own)
    return whole.reshape(count * rows, width)


def reduce(pairs, count, ident, regather):
    chips, rows, width = pairs[0][0].shape
    half = chips // 2
    dma = pltpu.SemaphoreType.DMA
    out_shape = [jax.ShapeDtypeStruct((rows, width), jnp.bfloat16) for _ in pairs]
    if regather:
        out_shape.append(jax.ShapeDtypeStruct((chips, 2, rows, width), jnp.bfloat16))
    scratch = []
    for _ in pairs:
        hop = (2, half, SUBS, rows // SUBS, width)
        scratch += [
            pltpu.VMEM((chips, rows, width), jnp.bfloat16),
            pltpu.VMEM(hop, jnp.bfloat16),
            pltpu.VMEM(hop, jnp.bfloat16),
            dma((2, half, SUBS)), dma((2, half, SUBS)), dma((chips,)), dma((chips,)),
        ]
    if regather:
        scratch += gather_scratch(count)
    return pl.pallas_call(
        functools.partial(reduce_kernel, count, len(pairs), regather),
        out_shape=out_shape,
        in_specs=[VM] * (2 * len(pairs)),
        out_specs=[VM] * len(out_shape),
        scratch_shapes=scratch,
        compiler_params=pltpu.CompilerParams(
            collective_id=ident, has_side_effects=True, vmem_limit_bytes=BIG
        ),
        name="reduce_rows_gather" if regather else "reduce_rows",
    )(*[ref for pair in pairs for ref in pair])


def apply_kernel(pair, limits, core, mixers, v_ref, l_ref, r_ref, own_ref, give_ref, acc):
    q = pl.program_id(0)
    terms = l_ref.shape[0]
    block = l_ref.shape[2]
    local = v_ref.shape[0] // block
    acc[...] = jnp.zeros_like(acc)
    for t in range(terms):
        @pl.when(q < limits[t])
        def _(t=t):
            left = l_ref[t, 0]
            right = r_ref[t, 0]
            lifted = [
                jnp.dot(left, v_ref[pl.ds(s * block, block), :], preferred_element_type=jnp.float32)
                .astype(jnp.bfloat16).astype(jnp.float32)
                for s in range(local)
            ]
            for x in range(local):
                mixed = mixers[t, x * local] * lifted[0]
                for y in range(1, local):
                    mixed = mixed + mixers[t, x * local + y] * lifted[y]
                rows = pl.ds(x * block, block)
                acc[rows, :] += lax.dot_general(
                    mixed.astype(jnp.bfloat16), right, (((1,), (1,)), ((), ())),
                    preferred_element_type=jnp.float32,
                )
    here = core[0]
    chips, rows, _ = own_ref.shape
    for j in range(chips):
        own_ref[j] = acc[pl.ds(pl.multiple_of((2 * j + here) * rows, rows), rows), :]
        give_ref[j] = acc[
            pl.ds(pl.multiple_of((2 * j + 1 - here) * rows, rows), rows), :
        ].astype(jnp.bfloat16)


def apply_local(whole, lefts, rights, mixers, limits, pair, core, count):
    terms, sectors, block, _ = lefts.shape
    rows_all, width = whole.shape
    height = rows_all // sectors
    chips = count // 2
    rows = rows_all // count
    each = chips // sectors
    mats = (terms, 1, block, block)
    grid_spec = pltpu.PrefetchScalarGridSpec(
        num_scalar_prefetch=4,
        grid=(sectors,),
        in_specs=[
            pl.BlockSpec((height, width), lambda q, *_: (q, 0)),
            pl.BlockSpec(mats, lambda q, *_: (0, q, 0, 0)),
            pl.BlockSpec(mats, lambda q, pair, *_: (0, pair[q], 0, 0)),
        ],
        out_specs=[pl.BlockSpec((each, rows, width), lambda q, *_: (q, 0, 0))] * 2,
        scratch_shapes=[pltpu.VMEM((height, width), jnp.float32)],
    )
    return pl.pallas_call(
        apply_kernel,
        grid_spec=grid_spec,
        out_shape=[
            jax.ShapeDtypeStruct((chips, rows, width), jnp.float32),
            jax.ShapeDtypeStruct((chips, rows, width), jnp.bfloat16),
        ],
        compiler_params=pltpu.CompilerParams(vmem_limit_bytes=BIG),
        cost_estimate=pl.CostEstimate(
            flops=4 * terms * rows_all * width * block, transcendentals=0,
            bytes_accessed=4 * lefts.size + 8 * rows_all * width,
        ),
        name="apply_terms",
    )(pair, limits, core, mixers, whole, lefts, rights)


def renew_kernel(back, l_ref, t_ref, out_ref):
    terms = l_ref.shape[0]
    local = t_ref.shape[1]
    for t in range(terms):
        total = None
        for s in range(local):
            lifted = jnp.dot(
                l_ref[t, 0], t_ref[0, s], preferred_element_type=jnp.float32
            ).astype(jnp.bfloat16)
            term = lax.dot_general(
                t_ref[0, s], lifted, (((0,), (0,)), ((), ())),
                preferred_element_type=jnp.float32,
            )
            total = term if total is None else total + term
        out_ref[t, 0] = total.astype(jnp.bfloat16)


def renew(lefts, tensor, pair):
    terms, sectors, block, _ = lefts.shape
    local = tensor.shape[1]
    ids = jnp.arange(sectors, dtype=jnp.int32)
    back = jnp.sum((pair[None, :] == ids[:, None]) * ids[None, :], axis=1).astype(jnp.int32)
    return pl.pallas_call(
        renew_kernel,
        grid_spec=pltpu.PrefetchScalarGridSpec(
            num_scalar_prefetch=1,
            grid=(sectors,),
            in_specs=[
                pl.BlockSpec((terms, 1, block, block), lambda j, back: (0, back[j], 0, 0)),
                pl.BlockSpec((1, local, block, block), lambda j, back: (back[j], 0, 0, 0)),
            ],
            out_specs=pl.BlockSpec((terms, 1, block, block), lambda j, back: (0, j, 0, 0)),
        ),
        out_shape=jax.ShapeDtypeStruct(lefts.shape, jnp.bfloat16),
        compiler_params=pltpu.CompilerParams(vmem_limit_bytes=BIG),
        cost_estimate=pl.CostEstimate(
            flops=4 * lefts.size * local * block, transcendentals=0,
            bytes_accessed=4 * lefts.size + 2 * tensor.size,
        ),
        name="renew",
    )(back, lefts, tensor)


def shards(count, wave, left_ops, right_ops, site_ops, reach, pairing, site_tensor):
    lefts, rights, limits, pair = left_ops[0], right_ops[0], reach[0], pairing[0]
    mixers = site_ops[0].reshape(site_ops.shape[1], -1)
    core = lax.rem(lax.axis_index("op"), 2).astype(jnp.int32).reshape(1)
    renewed = renew(lefts, site_tensor[0], pair)
    size = lax.axis_size("sect")
    moved_lefts = lax.ppermute(renewed, "sect", [(i, (i + 1) % size) for i in range(size)])
    whole = all_gather(wave[0], count, 0)
    part = apply_local(whole, lefts, rights, mixers, limits, pair, core, count)
    first_own, first_full = reduce([part], count, 1, True)
    first_full = first_full.reshape(whole.shape)
    moved_part = apply_local(whole, moved_lefts, rights, mixers, limits, pair, core, count)
    second_part = apply_local(first_full, lefts, rights, mixers, limits, pair, core, count)
    second_own, moved_own = reduce([second_part, moved_part], count, 2, False)
    return first_own[None], second_own[None], moved_own[None]


def solution(mesh):
    placed = (
        P("sect", "op", None),
        P("sect", "op", None, None, None),
        P("sect", "op", None, None, None),
        P("sect", "op", None, None),
        P("sect", "op"),
        P("sect", None),
        P("sect", None, None, None, None),
    )
    return jax.shard_map(
        functools.partial(shards, mesh.shape["op"]),
        mesh=mesh,
        in_specs=placed,
        out_specs=(P("sect", "op", None), P("sect", "op", None), P("sect", "op", None)),
        check_vma=False,
    )
```

time: 562 us -> 212 us (0.38)
  matrix products: 238 us -> 0 us
  waiting for transfers between devices: 228 us -> 0.01 us
  Pallas kernels: 0 us -> 199 us
  local copies, waits for them, and re-layouts: 63.4 us -> 4.71 us
  between operations: 14.2 us -> 0.67 us
  other arithmetic: 10.7 us -> 1.28 us
    dot_general x33 -> x0, matrix products: 238 us -> none  [the longest x9 99.7 us: apply_local(): jnp.einsum('xy,qyac->qxac', mixers[term], lifted.astype(jnp.float32), pre...]
    pallas_call x0 -> x7, Pallas kernels: none -> 199 us  [the longest x2 111 us: reduce(): pl.pallas_call(functools.partial(reduce_kernel, count, len(pairs), regath...]
    reduce_scatter x3 -> x0, waiting for transfers between devices: 178 us -> none  [the longest x1 105 us: shards(): lax.psum_scatter(second_part, 'op', scatter_dimension=0, tiled=True)]
    all_gather x2 -> x0, waiting for transfers between devices: 45.9 us -> none  [the longest x1 45.9 us: shards(): whole = lax.all_gather(wave[0], 'op', axis=0, tiled=True)]
    convert_element_type x6 -> x0, local copies, waits for them, and re-layouts: 45.1 us -> none  [apply_local(): lifted = jnp.einsum('qab,qsbc->qsac', lefts[term], blocks, preferred_elem...]
    dot_general x3 -> x0, local copies, waits for them, and re-layouts: 8.39 us -> none  [renew_boundary(): jnp.einsum('qsad,qsac->qdc', tensor, lifted, preferred_element_type=jnp.f...]
  transfers between devices with their start and end apart: 6 -> 1, of which waited for: 5 -> 0; matrix products, arithmetic and copies ran while one was open for 39% -> 0% of each run, Pallas kernels for 0% -> 57%
where the time goes in v1:
time: 212 us; the launch traced here: 209 us
  Pallas kernels  199 us (94%)
  local copies, waits for them, and re-layouts  4.71 us (2%)
  starting transfers between devices  3 us (1%)
    pallas_call x2, Pallas kernels, reduce(): pl.pallas_call(functools.partial(reduce_kernel, count, len(pairs), regath...  111 us
    pallas_call x3, Pallas kernels, apply_local(): pl.pallas_call(apply_kernel, grid_spec=grid_spec, out_shape=[jax.ShapeDty...  45.6 us
    pallas_call x1, Pallas kernels, all_gather(): pl.pallas_call(functools.partial(gather_kernel, count), out_shape=jax.Sha...  29.4 us
    pallas_call x1, Pallas kernels, renew(): pl.pallas_call(renew_kernel, grid_spec=pltpu.PrefetchScalarGridSpec(num_s...  12.8 us
  transfers between devices with their start and end apart: 1, of which 0 were waited for; matrix products, arithmetic and copies ran while one was open for 0% of the time, Pallas kernels for 57%

profile of v1, /device:TPU:0, one launch (start us, length us, event | category | flops | bytes accessed | tf_op | source)
XLA Modules:
  0.0 208.9 jit_solution(8090247613543651122)
XLA Ops:
  0.6 1.3 select_reduce_fusion.back
  1.9 0.0 copy-start.1
  1.9 12.8 %renew.1 = bf16[3,8,256,256]{3,2,1,0:T(8,128)(2,1)} custom-call(s32[8]{0:T(128)} %select_reduce_fusion.back, bf16[3,8,256,256]{3,2,1,0:T(8,128)(2,1)} %bitcast.20, bf16[8,4,256,256]{3,2,1,0:T(8,128)(2,1)} %bitcast.18), custom_call_target="tpu_custom_call" | custom-call | flops 6442450944 | bytes 10485760 | tf_op jit(solution)/shard_map/renew/pallas_call | solution.py:328
  14.8 3.0 %collective-permute-start = (bf16[3,8,256,256]{3,2,1,0:T(8,128)(2,1)}, bf16[3,8,256,256]{3,2,1,0:T(8,128)(2,1)}, u32[]{:S(2)}, u32[]{:S(2)}) collective-permute-start(bf16[3,8,256,256]{3,2,1,0:T(8,128)(2,1)} %renew.1), channel_id=1, source_target_pairs={{0,16},{16,0},{1,17},{17,1},{2,18},{18,2},{3,19},{19,3},{4,20},{20... | collective-permute-start | bytes 9437192 | tf_op jit(solution)/shard_map/ppermute | solution.py:355
  17.8 0.0 copy-done.1
  17.8 0.7 reshape_squeeze.3.mixers
  18.4 29.4 %gather_rows.1 = bf16[8,2,512,256]{3,2,1,0:T(8,128)(2,1)} custom-call(bf16[512,256]{1,0:T(8,128)(2,1)} %bitcast.14), custom_call_target="tpu_custom_call" | custom-call | tf_op jit(solution)/shard_map/gather_rows/pallas_call | solution.py:192
  47.9 15.2 %apply_terms.3 = (f32[8,512,256]{2,1,0:T(8,128)}, bf16[8,512,256]{2,1,0:T(8,128)(2,1)}) custom-call(s32[8]{0:T(128)} %bitcast.27, s32[3]{0:T(128)} %bitcast.30, s32[1]{0:T(128)} %bitcast.2.core, f32[3,16]{1,0:T(4,128)} %reshape_squeeze.3.mixers, bf16[8192,256]{1,0:T(8,128)(2,1)} %bitcast.12, bf16[3,8,256,256]{3,2,1,0:T(8,128)(2,1)} %bitcast.21, ...), custom_call_target="tpu_custom_call" | custom-call | flops 6442450944 | bytes 23068672 | tf_op jit(solution)/shard_map/apply_terms/pallas_call | solution.py:290
  63.1 58.6 %reduce_rows_gather.1 = (bf16[512,256]{1,0:T(8,128)(2,1)}, bf16[8,2,512,256]{3,2,1,0:T(8,128)(2,1)}) custom-call(f32[8,512,256]{2,1,0:T(8,128)} %get-tuple-element.13.refs_0_, bf16[8,512,256]{2,1,0:T(8,128)(2,1)} %get-tuple-element.14.refs_1_), custom_call_target="tpu_custom_call" | custom-call | tf_op jit(solution)/shard_map/reduce_rows_gather/pallas_call | solution.py:224
  121.7 15.2 %apply_terms.4 = (f32[8,512,256]{2,1,0:T(8,128)}, bf16[8,512,256]{2,1,0:T(8,128)(2,1)}) custom-call(s32[8]{0:T(128)} %bitcast.28, s32[3]{0:T(128)} %bitcast.31, s32[1]{0:T(128)} %bitcast.2.core, f32[3,16]{1,0:T(4,128)} %reshape_squeeze.3.mixers, bf16[8192,256]{1,0:T(8,128)(2,1)} %bitcast.19, bf16[3,8,256,256]{3,2,1,0:T(8,128)(2,1)} %bitcast.22, ...), custom_call_target="tpu_custom_call" | custom-call | flops 6442450944 | bytes 23068672 | tf_op jit(solution)/shard_map/apply_terms/pallas_call | solution.py:290
  136.9 0.0 collective-permute-done.l_ref
  136.9 15.2 %apply_terms.5 = (f32[8,512,256]{2,1,0:T(8,128)}, bf16[8,512,256]{2,1,0:T(8,128)(2,1)}) custom-call(s32[8]{0:T(128)} %bitcast.29, s32[3]{0:T(128)} %bitcast.32, s32[1]{0:T(128)} %bitcast.2.core, f32[3,16]{1,0:T(4,128)} %reshape_squeeze.3.mixers, bf16[8192,256]{1,0:T(8,128)(2,1)} %bitcast.13, bf16[3,8,256,256]{3,2,1,0:T(8,128)(2,1)} %collective-permute-done.l_ref, ...), custom_call_target="tpu_custom_call" | custom-call | flops 6442450944 | bytes 23068672 | tf_op jit(solution)/shard_map/apply_terms/pallas_call | solution.py:290
  152.1 0.0 copy-start
  152.1 52.7 %reduce_rows.1 = (bf16[512,256]{1,0:T(8,128)(2,1)}, bf16[512,256]{1,0:T(8,128)(2,1)}) custom-call(f32[8,512,256]{2,1,0:T(8,128)} %get-tuple-element.17.refs_0_, bf16[8,512,256]{2,1,0:T(8,128)(2,1)} %get-tuple-element.18.refs_1_, f32[8,512,256]{2,1,0:T(8,128)} %get-tuple-element.19.refs_2_, bf16[8,512,256]{2,1,0:T(8,128)(2,1)} %get-tuple-element.20.refs_3_), custom_call_target="tpu_custom_call" | custom-call | tf_op jit(solution)/shard_map/reduce_rows/pallas_call | solution.py:224
  204.8 0.0 copy-done
  204.8 0.7 copy.13
  205.5 1.7 copy.14
  207.2 1.7 copy.15
Async XLA Ops:
  1.9 15.9 %copy-start.1 = (f32[1,3,4,4]{3,2,1,0:T(4,128)S(1)}, f32[1,3,4,4]{3,2,1,0:T(4,128)}, u32[]{:S(2)}) copy-start(f32[1,3,4,4]{3,2,1,0:T(4,128)} %param.10) | copy-start | bytes 580
  14.8 122.1 %collective-permute-start = (bf16[3,8,256,256]{3,2,1,0:T(8,128)(2,1)}, bf16[3,8,256,256]{3,2,1,0:T(8,128)(2,1)}, u32[]{:S(2)}, u32[]{:S(2)}) collective-permute-start(bf16[3,8,256,256]{3,2,1,0:T(8,128)(2,1)} %renew.1), channel_id=1, source_target_pairs={{0,16},{16,0},{1,17},{17,1},{2,18},{18,2},{3,19},{19,3},{4,20},{20... | collective-permute-start | bytes 9437192 | tf_op jit(solution)/shard_map/ppermute | solution.py:355
  152.1 52.7 %copy-start = (bf16[512,256]{1,0:T(8,128)(2,1)S(1)}, bf16[512,256]{1,0:T(8,128)(2,1)}, u32[]{:S(2)}) copy-start(bf16[512,256]{1,0:T(8,128)(2,1)} %get-tuple-element.15) | copy-start | bytes 786436

commit v2 on v1

v2 whole, which is shorter than its diff:
```python
import functools

import jax
import jax.numpy as jnp
from jax import lax
from jax.experimental import pallas as pl
from jax.experimental.pallas import tpu as pltpu
from jax.sharding import PartitionSpec as P

VM = pl.BlockSpec(memory_space=pltpu.VMEM)
SUBS = 2
BIG = 64000 * 1024


class Ring:
    def __init__(self, count):
        me = lax.axis_index("op")
        self.m = count // 2
        self.half = self.m // 2
        self.core = lax.rem(me, 2)
        self.chip = lax.div(me, 2)
        odd = lax.rem(self.chip, 2)
        low = lax.div(self.chip, 2)
        self.pos = (1 - odd) * low + odd * (self.m - 1 - low)
        self.sibling = {"op": self.chip * 2 + 1 - self.core}
        self.next = [
            {"op": self.chip_at(1) * 2 + self.core},
            {"op": self.chip_at(-1) * 2 + self.core},
        ]

    def chip_at(self, offset):
        pos = lax.rem(self.pos + offset + self.m, self.m)
        upper = lax.div(pos, self.half)
        return (1 - upper) * (2 * pos) + upper * (2 * (self.m - 1 - pos) + 1)

    def barrier(self):
        sem = pltpu.get_barrier_semaphore()
        for who in (self.next[0], self.next[1], self.sibling):
            pl.semaphore_signal(sem, inc=1, device_id=who, device_id_type=pl.DeviceIdType.MESH)
        pl.semaphore_wait(sem, 3)


def push(src, dst, send, recv, who):
    copy = pltpu.make_async_remote_copy(
        src_ref=src, dst_ref=dst, send_sem=send, recv_sem=recv, device_id=who,
        device_id_type=pl.DeviceIdType.MESH,
    )
    copy.start()
    return copy


def scatter_sum(ring, streams, hook=lambda step: None):
    m, half = ring.m, ring.half
    order = [half]
    for dist in range(half - 1, 0, -1):
        order += [dist, -dist]
    order.append(0)
    sent = []
    sib = {}
    for slot, offset in enumerate(order):
        chunk = ring.chip_at(offset)
        for n, st in enumerate(streams):
            sib[n, offset] = push(
                st["give"].at[chunk], st["land"].at[chunk], st["sib_send"].at[slot],
                st["sib_recv"].at[slot], ring.sibling,
            )
    arrived = set()
    hops = {}

    def local(n, offset, u):
        st = streams[n]
        if (n, offset) not in arrived:
            arrived.add((n, offset))
            sib[n, offset].wait_recv()
        chunk = ring.chip_at(offset)
        rows = st["own"].shape[1] // SUBS
        cut = pl.ds(u * rows, rows)
        return st["own"][chunk, cut, :] + st["land"][chunk, cut, :].astype(jnp.float32)

    def incoming(n, d, j, u):
        hops[n, d, j, u].wait_recv()
        return streams[n]["rbuf"][d, j, u].astype(jnp.float32)

    for j in range(half):
        dist = half - j
        for n, st in enumerate(streams):
            for u in range(SUBS):
                for d in range(2):
                    if dist == half and u != d:
                        continue
                    offset = dist if (d == 0 or dist == half) else -dist
                    value = local(n, offset, u)
                    if (n, d, j - 1, u) in hops:
                        value = value + incoming(n, d, j - 1, u)
                    st["sbuf"][d, j, u] = value.astype(jnp.bfloat16)
                    hops[n, d, j, u] = push(
                        st["sbuf"].at[d, j, u], st["rbuf"].at[d, j, u],
                        st["send"].at[d, j, u], st["recv"].at[d, j, u], ring.next[d],
                    )
        hook(j)
    for n, st in enumerate(streams):
        for u in range(SUBS):
            value = local(n, 0, u)
            for d in range(2):
                if (n, d, half - 1, u) in hops:
                    value = value + incoming(n, d, half - 1, u)
            rows = value.shape[0]
            st["out"][pl.ds(u * rows, rows), :] = value.astype(jnp.bfloat16)
    sent += list(sib.values()) + list(hops.values())
    return sent


def gather(ring, own, whole, send, recv, sib_send, sib_recv, hook):
    half = ring.half
    each = ring.m // whole.shape[0]
    rows = own.shape[0] // SUBS
    sib, hops = [], {}

    def part(chunk, u):
        start = (lax.rem(chunk, each) * 2 + ring.core) * own.shape[0] + u * rows
        return whole.at[lax.div(chunk, each), pl.ds(pl.multiple_of(start, rows), rows)]

    for s in range(half + 1):
        first = len(sib)
        for u in range(SUBS):
            for d in range(2):
                chunk = ring.chip_at(-s if d == 0 else s)
                if s == 0:
                    src = own.at[pl.ds(u * rows, rows)]
                else:
                    if (d, s - 1, u) not in hops:
                        continue
                    hops[d, s - 1, u].wait_recv()
                    src = part(chunk, u)
                if s < half and (s < half - 1 or u == d):
                    hops[d, s, u] = push(
                        src, part(chunk, u), send.at[d, s, u], recv.at[d, s, u], ring.next[d]
                    )
                if s > 0 or d == 0:
                    slot = len(sib)
                    sib.append(push(
                        src, part(chunk, u), sib_send.at[slot], sib_recv.at[slot], ring.sibling
                    ))

        def ready(first=first, last=len(sib)):
            for copy in sib[first:last]:
                copy.wait_recv()

        hook(s, ready)
    return sib + list(hops.values())


def keep_own(ring, own, whole, sem):
    each = ring.m // whole.shape[0]
    start = (lax.rem(ring.chip, each) * 2 + ring.core) * own.shape[0]
    keep = pltpu.make_async_copy(
        own,
        whole.at[lax.div(ring.chip, each), pl.ds(pl.multiple_of(start, own.shape[0]), own.shape[0])],
        sem,
    )
    keep.start()
    return keep


def apply_sector(ring, q, v, lefts, rights, mixers, limits, pair, acc, own, give):
    terms, _, block, _ = lefts.shape
    local = v.shape[1] // block
    for t in range(terms):
        left = lefts[t, q]
        right = rights[t, pair[q]]
        lifted = [
            jnp.dot(left, v[q, pl.ds(s * block, block), :], preferred_element_type=jnp.float32)
            .astype(jnp.bfloat16).astype(jnp.float32)
            for s in range(local)
        ]
        live = jnp.where(q < limits[t], 1.0, 0.0).astype(jnp.float32)
        for x in range(local):
            mixed = (live * mixers[t, x * local]) * lifted[0]
            for y in range(1, local):
                mixed = mixed + (live * mixers[t, x * local + y]) * lifted[y]
            rows = pl.ds(x * block, block)
            term = lax.dot_general(
                mixed.astype(jnp.bfloat16), right, (((1,), (1,)), ((), ())),
                preferred_element_type=jnp.float32,
            )
            acc[rows, :] = term if t == 0 else acc[rows, :] + term
    rows = own.shape[1]
    each = own.shape[0] // lefts.shape[1]
    for j in range(each):
        mine = pl.multiple_of((2 * j + ring.core) * rows, rows)
        other = pl.multiple_of((2 * j + 1 - ring.core) * rows, rows)
        own[q * each + j] = acc[pl.ds(mine, rows), :]
        give[q * each + j] = acc[pl.ds(other, rows), :].astype(jnp.bfloat16)


def renew_sector(j, back, lefts, tensor, out):
    terms = lefts.shape[0]
    local = tensor.shape[1]
    source = back[j]
    for t in range(terms):
        total = None
        for s in range(local):
            lifted = jnp.dot(
                lefts[t, source], tensor[source, s], preferred_element_type=jnp.float32
            ).astype(jnp.bfloat16)
            term = lax.dot_general(
                tensor[source, s], lifted, (((0,), (0,)), ((), ())),
                preferred_element_type=jnp.float32,
            )
            total = term if total is None else total + term
        out[t, j] = total.astype(jnp.bfloat16)


def while_gathering(ring, sectors, compute, extra=lambda step: None):
    def hook(s, ready):
        extra(s)
        ready()
        if ring.m != sectors:
            if s == ring.half:
                lax.fori_loop(0, sectors, lambda i, c: compute(i) or c, 0)
        elif s == 0 or s == ring.half:
            compute(ring.chip_at(s))
        else:
            lax.fori_loop(0, 2, lambda i, c: compute(ring.chip_at(s * (1 - 2 * i))) or c, 0)

    return hook


def load_all(pairs, sems):
    copies = [pltpu.make_async_copy(a, b, sems.at[i]) for i, (a, b) in enumerate(pairs)]
    for copy in copies:
        copy.start()
    return copies


def first_kernel(
    count, pair, back, limits, mixers, wave, left_in, right_in, tensor_in,
    whole, own, give, renewed, lefts, rights, tensor, acc, loads, local_sem, *sems
):
    ring = Ring(count)
    loaded = load_all([(left_in, lefts), (tensor_in, tensor), (right_in, rights)], loads)
    keep = keep_own(ring, wave, whole, local_sem)
    ring.barrier()
    sectors = lefts.shape[1]
    per = -(-sectors // ring.half)

    def extra(s):
        if s == 0:
            for copy in loaded:
                copy.wait()
            keep.wait()
        low, high = min(s * per, sectors), min(s * per + per, sectors)
        if low < high:
            lax.fori_loop(
                low, high, lambda j, c: renew_sector(j, back, lefts, tensor, renewed) or c, 0
            )

    def compute(q):
        apply_sector(ring, q, whole, lefts, rights, mixers, limits, pair, acc, own, give)

    sent = gather(ring, wave, whole, *sems, while_gathering(ring, sectors, compute, extra))
    for copy in sent:
        copy.wait_send()


def stream_of(refs):
    return dict(zip(
        ("own", "give", "out", "land", "sbuf", "rbuf", "send", "recv", "sib_send", "sib_recv"), refs
    ))


def second_kernel(
    count, pair, limits, mixers, own1, give1, left_in, right_in,
    out, own, give, lefts, rights, whole, acc, loads, local_sem, *rest
):
    ring = Ring(count)
    loaded = load_all([(left_in, lefts), (right_in, rights)], loads)
    ring.barrier()
    sent = scatter_sum(ring, [stream_of((own1, give1, out) + rest[:7])])
    keep = keep_own(ring, out, whole, local_sem)

    def extra(s):
        if s == 0:
            for copy in loaded:
                copy.wait()
            keep.wait()

    def compute(q):
        apply_sector(ring, q, whole, lefts, rights, mixers, limits, pair, acc, own, give)

    sent += gather(ring, out, whole, *rest[7:], while_gathering(ring, lefts.shape[1], compute, extra))
    for copy in sent:
        copy.wait_send()


def third_kernel(
    count, pair, limits, mixers, own2, give2, whole_in, left_in, right_in,
    out2, out3, whole, lefts, rights, own3, give3, acc, loads, *rest
):
    ring = Ring(count)
    loaded = load_all([(left_in, lefts), (right_in, rights), (whole_in, whole)], loads)
    ring.barrier()
    sectors = lefts.shape[1]
    per = -(-sectors // ring.half)

    def hook(s):
        if s == 0:
            for copy in loaded:
                copy.wait()
        low, high = min(s * per, sectors), min(s * per + per, sectors)
        if low < high:
            def body(q, c):
                apply_sector(ring, q, whole, lefts, rights, mixers, limits, pair, acc, own3, give3)
                return c
            lax.fori_loop(low, high, body, 0)

    sent = scatter_sum(ring, [stream_of((own2, give2, out2) + rest[:7])], hook)
    sent += scatter_sum(ring, [stream_of((own3, give3, out3) + rest[7:])])
    for copy in sent:
        copy.wait_send()


def gather_scratch(count):
    half = count // 4
    dma = pltpu.SemaphoreType.DMA
    slots = SUBS * (2 * half)
    return [dma((2, half, SUBS)), dma((2, half, SUBS)), dma((slots,)), dma((slots,)), dma]


def stream_scratch(chips, rows, width):
    half = chips // 2
    dma = pltpu.SemaphoreType.DMA
    hop = (2, half, SUBS, rows // SUBS, width)
    return [
        pltpu.VMEM((chips, rows, width), jnp.bfloat16),
        pltpu.VMEM(hop, jnp.bfloat16),
        pltpu.VMEM(hop, jnp.bfloat16),
        dma((2, half, SUBS)), dma((2, half, SUBS)), dma((chips,)), dma((chips,)),
    ]


def call(kernel, count, ident, ins, outs, scratch, name):
    shapes, specs = zip(*ins)
    return pl.pallas_call(
        functools.partial(kernel, count),
        out_shape=outs,
        in_specs=specs,
        out_specs=[VM] * len(outs),
        scratch_shapes=scratch,
        compiler_params=pltpu.CompilerParams(
            collective_id=ident, has_side_effects=True, vmem_limit_bytes=BIG
        ),
        name=name,
    )(*shapes)


def shards(count, wave, left_ops, right_ops, site_ops, reach, pairing, site_tensor):
    lefts, rights, limits, pair = left_ops[0], right_ops[0], reach[0], pairing[0]
    mixers = site_ops[0].reshape(site_ops.shape[1], -1)
    own, tensor = wave[0], site_tensor[0]
    sectors, block = lefts.shape[1:3]
    ids = jnp.arange(sectors, dtype=jnp.int32)
    back = jnp.sum((pair[None, :] == ids[:, None]) * ids[None, :], axis=1).astype(jnp.int32)
    rows, width = own.shape
    chips = count // 2
    height = count * rows // sectors
    dma = pltpu.SemaphoreType.DMA
    sm = pl.BlockSpec(memory_space=pltpu.SMEM)
    anyw = pl.BlockSpec(memory_space=pl.ANY)
    bf, f32 = jnp.bfloat16, jnp.float32
    whole_shape = (sectors, height, width)
    part = [
        jax.ShapeDtypeStruct((chips, rows, width), f32),
        jax.ShapeDtypeStruct((chips, rows, width), bf),
    ]
    mine = jax.ShapeDtypeStruct((rows, width), bf)
    ops = [pltpu.VMEM(lefts.shape, bf), pltpu.VMEM(rights.shape, bf)]
    acc = pltpu.VMEM((height, width), f32)
    small = [(pair, sm), (limits, sm), (mixers, sm)]

    whole, own1, give1, renewed = call(
        first_kernel, count, 0,
        [(pair, sm), (back, sm), (limits, sm), (mixers, sm), (own, VM), (lefts, anyw),
         (rights, anyw), (tensor, anyw)],
        [jax.ShapeDtypeStruct(whole_shape, bf)] + part + [jax.ShapeDtypeStruct(lefts.shape, bf)],
        ops + [pltpu.VMEM(tensor.shape, bf), acc, dma((3,))] + gather_scratch(count)[-1:]
        + gather_scratch(count)[:-1],
        "gather_apply",
    )
    size = lax.axis_size("sect")
    moved_lefts = lax.ppermute(renewed, "sect", [(i, (i + 1) % size) for i in range(size)])
    first_own, own2, give2 = call(
        second_kernel, count, 1,
        small + [(own1, VM), (give1, VM), (lefts, anyw), (rights, anyw)],
        [mine] + part,
        ops + [pltpu.VMEM(whole_shape, bf), acc, dma((2,))] + gather_scratch(count)[-1:]
        + stream_scratch(chips, rows, width) + gather_scratch(count)[:-1],
        "reduce_gather_apply",
    )
    second_own, moved_own = call(
        third_kernel, count, 2,
        small + [(own2, VM), (give2, VM), (whole, anyw), (moved_lefts, anyw), (rights, anyw)],
        [mine, mine],
        [pltpu.VMEM(whole_shape, bf)] + ops + [pltpu.VMEM(p.shape, p.dtype) for p in part]
        + [acc, dma((3,))] + stream_scratch(chips, rows, width) * 2,
        "reduce_apply_reduce",
    )
    return first_own[None], second_own[None], moved_own[None]


def solution(mesh):
    placed = (
        P("sect", "op", None),
        P("sect", "op", None, None, None),
        P("sect", "op", None, None, None),
        P("sect", "op", None, None),
        P("sect", "op"),
        P("sect", None),
        P("sect", None, None, None, None),
    )
    return jax.shard_map(
        functools.partial(shards, mesh.shape["op"]),
        mesh=mesh,
        in_specs=placed,
        out_specs=(P("sect", "op", None), P("sect", "op", None), P("sect", "op", None)),
        check_vma=False,
    )
```

time: 212 us -> 174 us (0.82); the launches traced: 209 us -> 174 us
  Pallas kernels: 199 us -> 156 us
  waiting for transfers between devices: 0.01 us -> 8.38 us
    pallas_call x7 -> x3, Pallas kernels: 199 us -> 156 us  [call(): pl.pallas_call(functools.partial(kernel, count), out_shape=outs, in_specs...]
    ppermute x1, waiting for transfers between devices: 0.01 us -> 8.38 us  [shards(): lax.ppermute(renewed, 'sect', [(i, (i + 1) % size) for i in range(size)])]
  transfers between devices with their start and end apart: 1 -> 1, of which waited for: 0 -> 1; matrix products, arithmetic and copies ran while one was open for 0% -> 0% of each run, Pallas kernels for 57% -> 35%
where the time goes in v2:
time: 174 us
  Pallas kernels  156 us (90%)
  waiting for transfers between devices  8.38 us (5%)
  local copies, waits for them, and re-layouts  5.4 us (3%)
    pallas_call x3, Pallas kernels, call(): pl.pallas_call(functools.partial(kernel, count), out_shape=outs, in_specs...  156 us
    ppermute x1, waiting for transfers between devices, shards(): lax.ppermute(renewed, 'sect', [(i, (i + 1) % size) for i in range(size)])  8.38 us
    unnamed x5, local copies, waits for them, and re-layouts  4.05 us
  transfers between devices with their start and end apart: 1, of which 1 were waited for; matrix products, arithmetic and copies ran while one was open for 0% of the time, Pallas kernels for 35%

profile of v2, /device:TPU:0, one launch (start us, length us, event | category | flops | bytes accessed | tf_op | source)
XLA Modules:
  0.0 173.7 jit_solution(11962437483455058525)
XLA Ops:
  0.6 1.3 select_reduce_fusion.back
  1.9 1.4 reshape_squeeze.3.mixers
  3.3 37.9 %gather_apply.1 = (bf16[8,1024,256]{2,1,0:T(8,128)(2,1)}, f32[8,512,256]{2,1,0:T(8,128)}, bf16[8,512,256]{2,1,0:T(8,128)(2,1)}, bf16[3,8,256,256]{3,2,1,0:T(8,128)(2,1)}) custom-call(s32[8]{0:T(128)} %bitcast.20, s32[8]{0:T(128)} %select_reduce_fusion.back, s32[3]{0:T(128)} %bitcast.23, f32[3,16]{1,0:T(4,128)} %reshape_squeeze.3.mixers, ...), custom_call_target="tpu_custom_call" | custom-call | tf_op jit(solution)/shard_map/gather_apply/pallas_call | solution.py:344
  41.2 1.6 collective-permute-start
  42.8 61.1 %reduce_gather_apply.1 = (bf16[512,256]{1,0:T(8,128)(2,1)}, f32[8,512,256]{2,1,0:T(8,128)}, bf16[8,512,256]{2,1,0:T(8,128)(2,1)}) custom-call(s32[8]{0:T(128)} %bitcast.21, s32[3]{0:T(128)} %bitcast.24, f32[3,16]{1,0:T(4,128)} %reshape_squeeze.3.mixers, f32[8,512,256]{2,1,0:T(8,128)} %get-tuple-element.12.own1, ...), custom_call_target="tpu_custom_call" | custom-call | tf_op jit(solution)/shard_map/reduce_gather_apply/pallas_call | solution.py:344
  103.9 8.4 %collective-permute-done.left_in = bf16[3,8,256,256]{3,2,1,0:T(8,128)(2,1)} collective-permute-done((bf16[3,8,256,256]{3,2,1,0:T(8,128)(2,1)}, bf16[3,8,256,256]{3,2,1,0:T(8,128)(2,1)}, u32[]{:S(2)}, u32[]{:S(2)}) %collective-permute-start) | collective-permute-done | bytes 3145760 | tf_op jit(solution)/shard_map/ppermute | solution.py:391
  112.3 0.0 copy-start
  112.3 57.4 %reduce_apply_reduce.1 = (bf16[512,256]{1,0:T(8,128)(2,1)}, bf16[512,256]{1,0:T(8,128)(2,1)}) custom-call(s32[8]{0:T(128)} %bitcast.22, s32[3]{0:T(128)} %bitcast.25, f32[3,16]{1,0:T(4,128)} %reshape_squeeze.3.mixers, f32[8,512,256]{2,1,0:T(8,128)} %get-tuple-element.15.own2, bf16[8,512,256]{2,1,0:T(8,128)(2,1)} %get-tuple-element.16.give2, ...), custom_call_target="tpu_custom_call" | custom-call | tf_op jit(solution)/shard_map/reduce_apply_reduce/pallas_call | solution.py:344
  169.7 0.0 copy-done
  169.7 0.7 copy.13
  170.4 1.7 copy.14
  172.0 1.7 copy.15
Async XLA Ops:
  41.2 71.1 %collective-permute-start = (bf16[3,8,256,256]{3,2,1,0:T(8,128)(2,1)}, bf16[3,8,256,256]{3,2,1,0:T(8,128)(2,1)}, u32[]{:S(2)}, u32[]{:S(2)}) collective-permute-start(bf16[3,8,256,256]{3,2,1,0:T(8,128)(2,1)} %get-tuple-element.18), channel_id=1, source_target_pairs={{0,16},{16,0},{1,17},{17,1},{2,18},{18,2},{3,19},{19,3},{4,20},{20... | collective-permute-start | bytes 9437192 | tf_op jit(solution)/shard_map/ppermute | solution.py:391
  112.3 57.4 %copy-start = (bf16[512,256]{1,0:T(8,128)(2,1)S(1)}, bf16[512,256]{1,0:T(8,128)(2,1)}, u32[]{:S(2)}) copy-start(bf16[512,256]{1,0:T(8,128)(2,1)} %get-tuple-element.14) | copy-start | bytes 786436

commit v3 on v2

--- a/solution.py
+++ b/solution.py
@@ -9,12 +9,16 @@
 
 VM = pl.BlockSpec(memory_space=pltpu.VMEM)
 SUBS = 2
-BIG = 64000 * 1024
+BIG = 67043328
 
 
 class Ring:
-    def __init__(self, count):
+    def __init__(self, count, sections):
         me = lax.axis_index("op")
+        here = lax.axis_index("sect")
+        self.sections = sections
+        self.ahead = {"sect": lax.rem(here + 1, sections)}
+        self.behind = {"sect": lax.rem(here + sections - 1, sections)}
         self.m = count // 2
         self.half = self.m // 2
         self.core = lax.rem(me, 2)
@@ -35,9 +39,12 @@
 
     def barrier(self):
         sem = pltpu.get_barrier_semaphore()
-        for who in (self.next[0], self.next[1], self.sibling):
+        peers = [self.next[0], self.next[1], self.sibling, self.ahead]
+        if self.sections > 2:
+            peers.append(self.behind)
+        for who in peers:
             pl.semaphore_signal(sem, inc=1, device_id=who, device_id_type=pl.DeviceIdType.MESH)
-        pl.semaphore_wait(sem, 3)
+        pl.semaphore_wait(sem, len(peers))
 
 
 def push(src, dst, send, recv, who):
@@ -162,11 +169,11 @@
     return keep
 
 
-def apply_sector(ring, q, v, lefts, rights, mixers, limits, pair, acc, own, give):
-    terms, _, block, _ = lefts.shape
+def apply_sector(ring, q, v, left_of, rights, mixers, limits, pair, acc, own, give):
+    terms, sectors, block, _ = rights.shape
     local = v.shape[1] // block
     for t in range(terms):
-        left = lefts[t, q]
+        left = left_of(t, q)
         right = rights[t, pair[q]]
         lifted = [
             jnp.dot(left, v[q, pl.ds(s * block, block), :], preferred_element_type=jnp.float32)
@@ -185,7 +192,7 @@
             )
             acc[rows, :] = term if t == 0 else acc[rows, :] + term
     rows = own.shape[1]
-    each = own.shape[0] // lefts.shape[1]
+    each = own.shape[0] // sectors
     for j in range(each):
         mine = pl.multiple_of((2 * j + ring.core) * rows, rows)
         other = pl.multiple_of((2 * j + 1 - ring.core) * rows, rows)
@@ -208,7 +215,7 @@
                 preferred_element_type=jnp.float32,
             )
             total = term if total is None else total + term
-        out[t, j] = total.astype(jnp.bfloat16)
+        out[j, t] = total.astype(jnp.bfloat16)
 
 
 def while_gathering(ring, sectors, compute, extra=lambda step: None):
@@ -233,90 +240,96 @@
     return copies
 
 
-def first_kernel(
-    count, pair, back, limits, mixers, wave, left_in, right_in, tensor_in,
-    whole, own, give, renewed, lefts, rights, tensor, acc, loads, local_sem, *sems
+def stream_of(refs):
+    return dict(zip(
+        ("own", "give", "out", "land", "sbuf", "rbuf", "send", "recv", "sib_send", "sib_recv"), refs
+    ))
+
+
+def whole_kernel(
+    count, sections, pair, back, limits, mixers, wave, left_in, right_in, tensor_in,
+    out1, out2, out3,
+    lefts, rights, tensor, whole, image, renewed, moved, own_a, own_b, give1, give2, give3, acc,
+    loads, local_sem, ahead_send, ahead_recv, *rest
 ):
-    ring = Ring(count)
+    ring = Ring(count, sections)
     loaded = load_all([(left_in, lefts), (tensor_in, tensor), (right_in, rights)], loads)
-    keep = keep_own(ring, wave, whole, local_sem)
+    keep = keep_own(ring, wave, whole, local_sem.at[0])
     ring.barrier()
-    sectors = lefts.shape[1]
+    sectors = rights.shape[1]
     per = -(-sectors // ring.half)
-
-    def extra(s):
+    streams = [
+        stream_of((own, give, out) + rest[7 * i:7 * i + 7])
+        for i, (own, give, out) in enumerate(
+            ((own_a, give1, out1), (own_b, give2, out2), (own_a, give3, out3))
+        )
+    ]
+    gather_sems = rest[21:25], rest[25:29]
+    crossing = []
+
+    def span(s):
+        return min(s * per, sectors), min(s * per + per, sectors)
+
+    def renew_some(s):
         if s == 0:
             for copy in loaded:
                 copy.wait()
             keep.wait()
-        low, high = min(s * per, sectors), min(s * per + per, sectors)
+        low, high = span(s)
         if low < high:
             lax.fori_loop(
                 low, high, lambda j, c: renew_sector(j, back, lefts, tensor, renewed) or c, 0
             )
-
-    def compute(q):
-        apply_sector(ring, q, whole, lefts, rights, mixers, limits, pair, acc, own, give)
-
-    sent = gather(ring, wave, whole, *sems, while_gathering(ring, sectors, compute, extra))
-    for copy in sent:
-        copy.wait_send()
-
-
-def stream_of(refs):
-    return dict(zip(
-        ("own", "give", "out", "land", "sbuf", "rbuf", "send", "recv", "sib_send", "sib_recv"), refs
-    ))
-
-
-def second_kernel(
-    count, pair, limits, mixers, own1, give1, left_in, right_in,
-    out, own, give, lefts, rights, whole, acc, loads, local_sem, *rest
-):
-    ring = Ring(count)
-    loaded = load_all([(left_in, lefts), (right_in, rights)], loads)
-    ring.barrier()
-    sent = scatter_sum(ring, [stream_of((own1, give1, out) + rest[:7])])
-    keep = keep_own(ring, out, whole, local_sem)
-
-    def extra(s):
+        for j in range(low, high):
+            crossing.append(push(
+                renewed.at[j], moved.at[j], ahead_send.at[j], ahead_recv.at[j], ring.ahead
+            ))
+
+    def apply_first(q):
+        apply_sector(
+            ring, q, whole, lambda t, q: lefts[t, q], rights, mixers, limits, pair, acc,
+            own_a, give1,
+        )
+
+    def apply_second(q):
+        apply_sector(
+            ring, q, image, lambda t, q: lefts[t, q], rights, mixers, limits, pair, acc,
+            own_b, give2,
+        )
+
+    def apply_moved(s):
+        low, high = span(s)
+        for j in range(low, high):
+            crossing[j].wait_recv()
+
+        def body(q, c):
+            apply_sector(
+                ring, q, whole, lambda t, q: moved[q, t], rights, mixers, limits, pair, acc,
+                own_a, give3,
+            )
+            return c
+
+        if low < high:
+            lax.fori_loop(low, high, body, 0)
+
+    sent = gather(
+        ring, wave, whole, *gather_sems[0],
+        while_gathering(ring, sectors, apply_first, renew_some),
+    )
+    sent += scatter_sum(ring, streams[:1])
+    kept = keep_own(ring, out1, image, local_sem.at[1])
+
+    def settle(s):
         if s == 0:
-            for copy in loaded:
-                copy.wait()
-            keep.wait()
-
-    def compute(q):
-        apply_sector(ring, q, whole, lefts, rights, mixers, limits, pair, acc, own, give)
-
-    sent += gather(ring, out, whole, *rest[7:], while_gathering(ring, lefts.shape[1], compute, extra))
-    for copy in sent:
-        copy.wait_send()
-
-
-def third_kernel(
-    count, pair, limits, mixers, own2, give2, whole_in, left_in, right_in,
-    out2, out3, whole, lefts, rights, own3, give3, acc, loads, *rest
-):
-    ring = Ring(count)
-    loaded = load_all([(left_in, lefts), (right_in, rights), (whole_in, whole)], loads)
-    ring.barrier()
-    sectors = lefts.shape[1]
-    per = -(-sectors // ring.half)
-
-    def hook(s):
-        if s == 0:
-            for copy in loaded:
-                copy.wait()
-        low, high = min(s * per, sectors), min(s * per + per, sectors)
-        if low < high:
-            def body(q, c):
-                apply_sector(ring, q, whole, lefts, rights, mixers, limits, pair, acc, own3, give3)
-                return c
-            lax.fori_loop(low, high, body, 0)
-
-    sent = scatter_sum(ring, [stream_of((own2, give2, out2) + rest[:7])], hook)
-    sent += scatter_sum(ring, [stream_of((own3, give3, out3) + rest[7:])])
-    for copy in sent:
+            kept.wait()
+
+    sent += gather(
+        ring, out1, image, *gather_sems[1],
+        while_gathering(ring, sectors, apply_second, settle),
+    )
+    sent += scatter_sum(ring, streams[1:2], apply_moved)
+    sent += scatter_sum(ring, streams[2:])
+    for copy in sent + crossing:
         copy.wait_send()
 
 
@@ -324,7 +337,7 @@
     half = count // 4
     dma = pltpu.SemaphoreType.DMA
     slots = SUBS * (2 * half)
-    return [dma((2, half, SUBS)), dma((2, half, SUBS)), dma((slots,)), dma((slots,)), dma]
+    return [dma((2, half, SUBS)), dma((2, half, SUBS)), dma((slots,)), dma((slots,))]
 
 
 def stream_scratch(chips, rows, width):
@@ -339,22 +352,7 @@
     ]
 
 
-def call(kernel, count, ident, ins, outs, scratch, name):
-    shapes, specs = zip(*ins)
-    return pl.pallas_call(
-        functools.partial(kernel, count),
-        out_shape=outs,
-        in_specs=specs,
-        out_specs=[VM] * len(outs),
-        scratch_shapes=scratch,
-        compiler_params=pltpu.CompilerParams(
-            collective_id=ident, has_side_effects=True, vmem_limit_bytes=BIG
-        ),
-        name=name,
-    )(*shapes)
-
-
-def shards(count, wave, left_ops, right_ops, site_ops, reach, pairing, site_tensor):
+def shards(count, sections, wave, left_ops, right_ops, site_ops, reach, pairing, site_tensor):
     lefts, rights, limits, pair = left_ops[0], right_ops[0], reach[0], pairing[0]
     mixers = site_ops[0].reshape(site_ops.shape[1], -1)
     own, tensor = wave[0], site_tensor[0]
@@ -368,44 +366,28 @@
     sm = pl.BlockSpec(memory_space=pltpu.SMEM)
     anyw = pl.BlockSpec(memory_space=pl.ANY)
     bf, f32 = jnp.bfloat16, jnp.float32
-    whole_shape = (sectors, height, width)
-    part = [
-        jax.ShapeDtypeStruct((chips, rows, width), f32),
-        jax.ShapeDtypeStruct((chips, rows, width), bf),
-    ]
+    image = pltpu.VMEM((sectors, height, width), bf)
+    total = pltpu.VMEM((chips, rows, width), f32)
+    give = pltpu.VMEM((chips, rows, width), bf)
+    across = pltpu.VMEM((sectors, lefts.shape[0], block, block), bf)
     mine = jax.ShapeDtypeStruct((rows, width), bf)
-    ops = [pltpu.VMEM(lefts.shape, bf), pltpu.VMEM(rights.shape, bf)]
-    acc = pltpu.VMEM((height, width), f32)
-    small = [(pair, sm), (limits, sm), (mixers, sm)]
-
-    whole, own1, give1, renewed = call(
-        first_kernel, count, 0,
-        [(pair, sm), (back, sm), (limits, sm), (mixers, sm), (own, VM), (lefts, anyw),
-         (rights, anyw), (tensor, anyw)],
-        [jax.ShapeDtypeStruct(whole_shape, bf)] + part + [jax.ShapeDtypeStruct(lefts.shape, bf)],
-        ops + [pltpu.VMEM(tensor.shape, bf), acc, dma((3,))] + gather_scratch(count)[-1:]
-        + gather_scratch(count)[:-1],
-        "gather_apply",
-    )
-    size = lax.axis_size("sect")
-    moved_lefts = lax.ppermute(renewed, "sect", [(i, (i + 1) % size) for i in range(size)])
-    first_own, own2, give2 = call(
-        second_kernel, count, 1,
-        small + [(own1, VM), (give1, VM), (lefts, anyw), (rights, anyw)],
-        [mine] + part,
-        ops + [pltpu.VMEM(whole_shape, bf), acc, dma((2,))] + gather_scratch(count)[-1:]
-        + stream_scratch(chips, rows, width) + gather_scratch(count)[:-1],
-        "reduce_gather_apply",
-    )
-    second_own, moved_own = call(
-        third_kernel, count, 2,
-        small + [(own2, VM), (give2, VM), (whole, anyw), (moved_lefts, anyw), (rights, anyw)],
-        [mine, mine],
-        [pltpu.VMEM(whole_shape, bf)] + ops + [pltpu.VMEM(p.shape, p.dtype) for p in part]
-        + [acc, dma((3,))] + stream_scratch(chips, rows, width) * 2,
-        "reduce_apply_reduce",
-    )
-    return first_own[None], second_own[None], moved_own[None]
+    outs = pl.pallas_call(
+        functools.partial(whole_kernel, count, sections),
+        out_shape=[mine] * 3,
+        in_specs=[sm] * 4 + [VM] + [anyw] * 3,
+        out_specs=[VM] * 3,
+        scratch_shapes=[
+            pltpu.VMEM(lefts.shape, bf), pltpu.VMEM(rights.shape, bf),
+            pltpu.VMEM(tensor.shape, bf), image, image, across, across, total, total,
+            give, give, give, pltpu.VMEM((height, width), f32),
+            dma((3,)), dma((2,)), dma((sectors,)), dma((sectors,)),
+        ] + stream_scratch(chips, rows, width) * 3 + gather_scratch(count) * 2,
+        compiler_params=pltpu.CompilerParams(
+            collective_id=0, has_side_effects=True, vmem_limit_bytes=BIG
+        ),
+        name="images",
+    )(pair, back, limits, mixers, own, lefts, rights, tensor)
+    return tuple(out[None] for out in outs)
 
 
 def solution(mesh):
@@ -419,7 +401,7 @@
         P("sect", None, None, None, None),
     )
     return jax.shard_map(
-        functools.partial(shards, mesh.shape["op"]),
+        functools.partial(shards, mesh.shape["op"], mesh.shape["sect"]),
         mesh=mesh,
         in_specs=placed,
         out_specs=(P("sect", "op", None), P("sect", "op", None), P("sect", "op", None)),

time: 174 us -> 144 us (0.83)
  Pallas kernels: 156 us -> 136 us
  waiting for transfers between devices: 8.38 us -> 0 us
    pallas_call x3 -> x1, Pallas kernels: 156 us -> 136 us  [shards(): pl.pallas_call(functools.partial(whole_kernel, count, sections), out_shap...]
    ppermute x1 -> x0, waiting for transfers between devices: 8.38 us -> none  [shards(): lax.ppermute(renewed, 'sect', [(i, (i + 1) % size) for i in range(size)])]
    unnamed x5 -> x3, local copies, waits for them, and re-layouts: 4.05 us -> 5.01 us
  transfers between devices with their start and end apart: 1 -> 0, of which waited for: 1 -> 0; matrix products, arithmetic and copies ran while one was open for 0% -> 0% of each run, Pallas kernels for 35% -> 0%
where the time goes in v3:
time: 144 us
  Pallas kernels  136 us (94%)
  local copies, waits for them, and re-layouts  6.36 us (4%)
    pallas_call x1, Pallas kernels, shards(): pl.pallas_call(functools.partial(whole_kernel, count, sections), out_shap...  136 us
    unnamed x3, local copies, waits for them, and re-layouts  5.01 us

profile of v3, /device:TPU:0, one launch (start us, length us, event | category | flops | bytes accessed | tf_op | source)
XLA Modules:
  0.0 144.1 jit_solution(2264711875962179009)
XLA Ops:
  0.6 1.3 select_reduce_fusion.back
  1.9 1.4 reshape_squeeze.3.mixers
  3.3 135.8 %images.1 = (bf16[512,256]{1,0:T(8,128)(2,1)}, bf16[512,256]{1,0:T(8,128)(2,1)}, bf16[512,256]{1,0:T(8,128)(2,1)}) custom-call(s32[8]{0:T(128)} %bitcast.17, s32[8]{0:T(128)} %select_reduce_fusion.back, s32[3]{0:T(128)} %bitcast.18, f32[3,16]{1,0:T(4,128)} %reshape_squeeze.3.mixers, bf16[512,256]{1,0:T(8,128)(2,1)} %bitcast.12, ...), custom_call_target="tpu_custom_call" | custom-call | tf_op jit(solution)/shard_map/images/pallas_call | solution.py:374
  139.1 1.7 %copy.13 = bf16[1,512,256]{2,1,0:T(8,128)(2,1)} copy(bf16[1,512,256]{2,1,0:T(8,128)(2,1)} %bitcast.15) | data formatting | bytes 524288
  140.7 1.7 %copy.14 = bf16[1,512,256]{2,1,0:T(8,128)(2,1)} copy(bf16[1,512,256]{2,1,0:T(8,128)(2,1)} %bitcast.14) | data formatting | bytes 524288
  142.4 1.7 %copy.15 = bf16[1,512,256]{2,1,0:T(8,128)(2,1)} copy(bf16[1,512,256]{2,1,0:T(8,128)(2,1)} %bitcast.13) | data formatting | bytes 524288
